TPU v7x, 512 devices: a whole 4x8x8 slice. The times are simulated.
512 devices in a mesh: dom: 128 (over z, y, core), rep: 4 (over x).
Axes of the slice: x: 4, y: 8, z: 8, core: 2. Of those that a mesh axis runs over, the one named last changes fastest.
Arguments:
- embedding: bfloat16 [131072, 128], P('dom'), may hold values from -6 to 6
- cotangent: bfloat16 [131072, 128], P('dom'), may hold values from -6 to 6
- degrees: int32 [131072], P('dom'), may hold values from 2 to 64
- tile_values: bfloat16 [128, 4, 32, 128, 128], P('dom', 'rep'), may hold values from 0 to 2, as said below
- tile_target: int32 [128, 4, 32], P('dom', 'rep'), may hold values from 0 to 7
- tile_source: int32 [128, 4, 32], P('dom', 'rep'), may hold values from 0 to 27
- live_tile_count: int32 [128, 4], P('dom', 'rep'), may hold values from 4 to 32, as said below
- send_rows: int32 [128, 128, 16], P('dom'), may hold values from 0 to 1023
- hub_rows: int32 [128, 4], P('dom'), may hold values from 0 to 1023
Outputs:
- layer_output: bfloat16 [131072, 128], P(('dom', 'rep'))
- embedding_gradient: bfloat16 [131072, 128], P(('dom', 'rep'))
Inputs may be any that keep to these rules, and one draw needn't show every extreme that they name: `tile_values`: each entry is an edge weight, zero where the two nodes share no edge. `live_tile_count`: slots at or past a device's count are not live; in every draw some device has all 32 slots live.
All inputs are finite; a program needn't handle non-finite values.
Results may differ from a plain program's by a relative error of at most 0.0048.
Values may be sent and summed in bfloat16 or wider, within the bound.
No kernel may reach another device: no remote copies, remote signals or barrier semaphores. Data moves between devices by JAX's collectives and lax.ppermute only.
A program may use at most 64 MiB of HBM per device.

v0:
```python
import jax
import jax.numpy as jnp
from jax import lax
from jax.sharding import PartitionSpec as P


def body(
    embedding,
    cotangent,
    degrees,
    tile_values,
    tile_target,
    tile_source,
    live_tile_count,
    send_rows,
    hub_rows,
):
    own_rows, feature_width = embedding.shape
    tile_size = tile_values.shape[-1]
    slot_grand_total = tile_values.shape[2]
    partitions = send_rows.shape[1]
    pair_rows = send_rows.shape[2]
    replicas = lax.axis_size("rep")
    replica_index = lax.axis_index("rep")
    root_inverse = lax.rsqrt(degrees.astype(jnp.float32))
    scaled = (root_inverse[:, None] * embedding.astype(jnp.float32)).astype(jnp.bfloat16)
    weighted = (root_inverse[:, None] * cotangent.astype(jnp.float32)).astype(jnp.bfloat16)
    arrived = lax.all_to_all(scaled[send_rows[0]], "dom", split_axis=0, concat_axis=0, tiled=True)
    hub_block = lax.all_gather(scaled[hub_rows[0]], "dom", axis=0, tiled=True)
    source = jnp.concatenate([scaled, arrived.reshape(-1, feature_width), hub_block], 0)
    source_blocks = source.shape[0] // tile_size
    source = source.reshape(source_blocks, tile_size, feature_width)
    target_blocks = own_rows // tile_size
    tile_matrix_block = tile_values[0, 0]
    targets = tile_target[0, 0]
    sources = tile_source[0, 0]
    tile_alive_mask = (
        jnp.arange(slot_grand_total, dtype=jnp.int32) < live_tile_count[0, 0]
    ).astype(jnp.float32)
    message_product = jnp.einsum(
        "ack,aky->acy", tile_matrix_block, source[sources], preferred_element_type=jnp.float32
    )
    target_onehot = (
        targets[None, :] == jnp.arange(target_blocks, dtype=jnp.int32)[:, None]
    ).astype(jnp.float32) * tile_alive_mask[None, :]
    forward = jnp.dot(
        target_onehot,
        message_product.reshape(slot_grand_total, -1),
        precision=lax.Precision.HIGHEST,
    )
    forward = forward.reshape(own_rows, feature_width)
    weighted_blocks = weighted.reshape(target_blocks, tile_size, feature_width)
    gathered_portion = jnp.einsum(
        "vzr,vzu->vru",
        tile_matrix_block,
        weighted_blocks[targets],
        preferred_element_type=jnp.float32,
    )
    source_onehot = (
        sources[None, :] == jnp.arange(source_blocks, dtype=jnp.int32)[:, None]
    ).astype(jnp.float32) * tile_alive_mask[None, :]
    slot_sums = jnp.dot(
        source_onehot,
        gathered_portion.reshape(slot_grand_total, -1),
        precision=lax.Precision.HIGHEST,
    )
    slot_sums = slot_sums.reshape(-1, feature_width)
    boundary_end = own_rows + partitions * pair_rows
    local_part = slot_sums[:own_rows]
    boundary_part = slot_sums[own_rows:boundary_end].reshape(partitions, pair_rows, feature_width)
    hub_part = slot_sums[boundary_end:]
    returned = lax.all_to_all(boundary_part, "dom", split_axis=0, concat_axis=0, tiled=True)
    gradient_part = local_part.at[send_rows[0]].add(returned)
    hub_total = lax.psum_scatter(hub_part, "dom", scatter_dimension=0, tiled=True)
    gradient_part = gradient_part.at[hub_rows[0]].add(hub_total)
    forward_sum, gradient_sum = (
        lax.psum_scatter(forward, "rep", scatter_dimension=0, tiled=True),
        lax.psum_scatter(gradient_part, "rep", scatter_dimension=0, tiled=True),
    )
    out_rows = own_rows // replicas
    my_root = lax.dynamic_slice_in_dim(root_inverse, replica_index * out_rows, out_rows, 0)
    layer_output = (my_root[:, None] * forward_sum).astype(jnp.bfloat16)
    embedding_gradient = (my_root[:, None] * gradient_sum).astype(jnp.bfloat16)
    return (layer_output, embedding_gradient)


def solution(mesh):
    placed = (
        P("dom", None),
        P("dom", None),
        P("dom"),
        P("dom", "rep", None, None, None),
        P("dom", "rep", None),
        P("dom", "rep", None),
        P("dom", "rep"),
        P("dom", None, None),
        P("dom", None),
    )
    return jax.shard_map(
        body,
        mesh=mesh,
        in_specs=placed,
        out_specs=(P(("dom", "rep"), None), P(("dom", "rep"), None)),
        check_vma=False,
    )
```

profile of v0, /device:TPU:8, one launch (start us, length us, event | category | flops | bytes accessed | tf_op | source)
XLA Modules:
  0.0 282.8 jit_solution(11773690477429332172)
XLA Ops:
  8.0 0.8 convert_rsqrt_fusion
  8.8 0.7 compare_select_fusion
  9.5 0.1 copy.16
  9.7 1.2 multiply_convert_fusion
  10.9 8.0 %gather_fusion = bf16[2048,128]{1,0:T(8,128)(2,1)} fusion(bf16[1024,128]{1,0:T(8,128)(2,1)S(1)} %get-tuple-element.3, s32[2048]{0:T(1024)S(1)} %broadcast_clamp_fusion), kind=kCustom, calls=%fused_computation | custom fusion | bytes 1056768 | tf_op jit(solution)/shard_map/gather | solution.py:28
  19.0 17.8 %all-to-all-start = ((bf16[128,16,128]{2,1,0:T(8,128)(2,1)}), bf16[128,16,128]{2,1,0:T(8,128)(2,1)}, u32[]{:S(2)}, u32[]{:S(2)}) async-start(bf16[128,16,128]{2,1,0:T(8,128)(2,1)} %bitcast.3), calls=%async_computation | async-start | bytes 1048576 | tf_op jit(solution)/shard_map/all_to_all | solution.py:28
  37.5 0.7 gather_fusion.3
  38.3 1.9 convolution_bitcast_fusion
  40.2 1.9 copy.20
  42.1 3.0 %fusion = f32[28,16384]{1,0:T(8,128)S(1)} fusion(f32[4,8,128,128]{3,2,1,0:T(8,128)S(1)} %bitcast.47, f32[32]{0:T(128)S(1)} %compare_convert_fusion, s32[32]{0:T(128)S(1)} %bitcast.53), kind=kOutput, calls=%fused_computation.6 | convolution fusion | flops 176162560 | bytes 3932416 | tf_op jit(solution)/shard_map/dot_general | solution.py:62
  45.1 1.3 copy-done.2
  46.5 0.9 slice.20
  47.4 0.4 slice-done
  47.8 1.1 reshape.157
  48.9 0.6 gather_fusion.1
  49.5 50.6 %all-gather.1 = bf16[128,4,128]{2,1,0:T(4,128)(2,1)S(1)} all-gather(bf16[1,4,128]{2,1,0:T(4,128)(2,1)S(1)} %bitcast.52), channel_id=2, replica_groups=mesh['dom'=128,'rep'=4] {'dom'}, dimensions={0}, use_global_device_ids=true | all-gather | bytes 132096 | tf_op jit(solution)/shard_map/all_gather | solution.py:29
  100.2 11.0 %all-to-all-start.1 = ((f32[128,16,128]{2,1,0:T(8,128)}), f32[128,16,128]{2,1,0:T(8,128)}, u32[]{:S(2)}, u32[]{:S(2)}) async-start(f32[128,16,128]{2,1,0:T(8,128)} %reshape.157), calls=%async_computation.2 | async-start | bytes 2097152 | tf_op jit(solution)/shard_map/all_to_all | solution.py:72
  111.2 0.2 reduce-scatter.3.cloned.1.call-start
  111.4 1.1 pad_maximum_fusion
  112.5 0.7 gather_fusion.2
  113.3 2.2 convolution_bitcast_fusion.1
  115.5 1.9 copy.18
  117.4 3.0 %fusion.3 = f32[8,16384]{1,0:T(8,128)} fusion(f32[4,8,128,128]{3,2,1,0:T(8,128)S(1)} %bitcast.48, f32[32]{0:T(128)S(1)} %compare_convert_fusion, s32[32]{0:T(128)S(1)} %bitcast.54), kind=kOutput, calls=%fused_computation.9 | convolution fusion | flops 50332160 | bytes 2621696 | tf_op jit(solution)/shard_map/dot_general | solution.py:46
  120.4 2.0 reshape.154
  122.6 1.3 dynamic-slice
  124.5 18.1 %all-to-all-done.1 = f32[128,16,128]{2,1,0:T(8,128)} async-done(((f32[128,16,128]{2,1,0:T(8,128)}), f32[128,16,128]{2,1,0:T(8,128)}, u32[]{:S(2)}, u32[]{:S(2)}) %all-to-all-start.1) | async-done | bytes 1048608 | tf_op jit(solution)/shard_map/all_to_all | solution.py:72
  142.6 12.0 %scatter_fusion = f32[1024,128]{1,0:T(8,128)S(1)} fusion(f32[1024,128]{1,0:T(8,128)S(1)} %slice.17, s32[2048]{0:T(1024)S(1)} %reshape.160, f32[2048,128]{1,0:T(8,128)} %bitcast.19), kind=kCustom, calls=%fused_computation.4 | custom fusion | flops 262144 | bytes 3153920 | tf_op jit(solution)/shard_map/scatter-add | solution.py:73
  154.7 92.1 %all-reduce.3.cloned.1.call-done = f32[512,128]{1,0:T(8,128)} async-done(((f32[512,128]{1,0:T(8,128)}), f32[512,128]{1,0:T(8,128)}) %all-reduce.3.cloned.1.call-update) | async-done | bytes 262160
  246.7 1.0 scatter_custom_fusion.1
  247.7 0.8 copy-done.1
  248.6 25.0 %reduce-scatter.5.cloned.1.call-done = f32[256,128]{1,0:T(8,128)} async-done(((f32[1024,128]{1,0:T(8,128)}), f32[256,128]{1,0:T(8,128)}) %reduce-scatter.5.cloned.1.call-update) | async-done | bytes 131088 | tf_op jit(solution)/shard_map/reduce_scatter | solution.py:78
  273.7 1.7 multiply_convert_fusion.2
  (32 shorter events, 0.5 us)
Async XLA Ops:
  8.0 30.3 %copy-start = (bf16[1,1,32,128,128]{4,3,2,1,0:T(8,128)(2,1)S(1)}, bf16[1,1,32,128,128]{4,3,2,1,0:T(8,128)(2,1)}, u32[]{:S(2)}) copy-start(bf16[1,1,32,128,128]{4,3,2,1,0:T(8,128)(2,1)} %param.12) | copy-start | bytes 3145732
  10.9 25.9 %copy-start.4 = (s32[1,1,32]{2,1,0:T(1,128)S(1)}, s32[1,1,32]{2,1,0:T(1,128)}, u32[]{:S(2)}) copy-start(s32[1,1,32]{2,1,0:T(1,128)} %param.13) | copy-start | bytes 388
  19.0 81.2 %all-to-all-start = ((bf16[128,16,128]{2,1,0:T(8,128)(2,1)}), bf16[128,16,128]{2,1,0:T(8,128)(2,1)}, u32[]{:S(2)}, u32[]{:S(2)}) async-start(bf16[128,16,128]{2,1,0:T(8,128)(2,1)} %bitcast.3), calls=%async_computation | async-start | bytes 1048576 | tf_op jit(solution)/shard_map/all_to_all | solution.py:28
  36.8 210.0 %all-reduce.3.cloned.1.call-start = ((), (), s32[]{:S(2)}) async-start(), calls=%async_computation.6 | async-start | bytes 524288
  40.2 1.9 copy-start.3
  45.1 1.3 copy-start.2
  46.5 1.3 slice-start
  47.4 1.5 copy-start.5
  100.2 42.5 %all-to-all-start.1 = ((f32[128,16,128]{2,1,0:T(8,128)}), f32[128,16,128]{2,1,0:T(8,128)}, u32[]{:S(2)}, u32[]{:S(2)}) async-start(f32[128,16,128]{2,1,0:T(8,128)} %reshape.157), calls=%async_computation.2 | async-start | bytes 2097152 | tf_op jit(solution)/shard_map/all_to_all | solution.py:72
  111.2 137.4 %reduce-scatter.3.cloned.1.call-start = ((), (), s32[]{:S(2)}) async-start(), calls=%async_computation.4 | async-start | bytes 655360 | tf_op jit(solution)/shard_map/reduce_scatter | solution.py:77
  120.4 2.1 slice-start.1
  122.5 151.2 %reduce-scatter.5.cloned.1.call-start = ((), (), s32[]{:S(2)}) async-start(), calls=%async_computation.5 | async-start | bytes 655360 | tf_op jit(solution)/shard_map/reduce_scatter | solution.py:78
  247.7 0.8 copy-start.1
Sparse Core Ops, SparseCore 0:
  47.5 199.1 all-reduce.2
Sparse Core Ops, SparseCore 1:
  122.5 27.8 reduce-scatter.2
  248.6 25.0 reduce-scatter.4
where the time goes:
time: 283 us
  waiting for transfers between devices  135 us (48%)
  blocking collectives  50.6 us (18%)
  starting transfers between devices  29.1 us (10%)
  local copies, waits for them, and re-layouts  22.1 us (8%)
  other arithmetic  18.6 us (7%)
  between operations  17 us (6%)
  matrix products  10.1 us (4%)
    unnamed x4, waiting for transfers between devices  92.1 us
    all_gather x1, blocking collectives, body(): hub_block = lax.all_gather(scaled[hub_rows[0]], 'dom', axis=0, tiled=True)  50.6 us
    reduce_scatter x1, waiting for transfers between devices, body(): lax.psum_scatter(gradient_part, 'rep', scatter_dimension=0, tiled=True)  25 us
    all_to_all x1, waiting for transfers between devices, body(): lax.all_to_all(boundary_part, 'dom', split_axis=0, concat_axis=0, tiled=T...  18.1 us
    all_to_all x1, starting transfers between devices, body(): lax.all_to_all(scaled[send_rows[0]], 'dom', split_axis=0, concat_axis=0,...  17.8 us
    scatter-add x1, other arithmetic, body(): gradient_part = local_part.at[send_rows[0]].add(returned)  12 us
    all_to_all x1, starting transfers between devices, body(): lax.all_to_all(boundary_part, 'dom', split_axis=0, concat_axis=0, tiled=T...  11 us
    gather x1, local copies, waits for them, and re-layouts, body(): scaled[send_rows[0]]  8.02 us
  transfers between devices with their start and end apart: 5, of which 3 were waited for; matrix products, arithmetic and copies ran while one was open for 13% of the time, Pallas kernels for 0%

commit v1 on v0

--- a/solution.py
+++ b/solution.py
@@ -1,7 +1,20 @@
+import functools
 import jax
 import jax.numpy as jnp
 from jax import lax
 from jax.sharding import PartitionSpec as P
+
+
+def edit_figure(original, lane_axis):
+    return jnp.concatenate(
+        lax.all_to_all(
+            jnp.stack([original for _ in range(lax.axis_size(lane_axis))], 0), lane_axis, 0, 0
+        ),
+        0,
+    )
+
+
+cube_test = functools.partial(edit_figure, lane_axis="dom")
 
 
 def body(
@@ -26,7 +39,7 @@
     scaled = (root_inverse[:, None] * embedding.astype(jnp.float32)).astype(jnp.bfloat16)
     weighted = (root_inverse[:, None] * cotangent.astype(jnp.float32)).astype(jnp.bfloat16)
     arrived = lax.all_to_all(scaled[send_rows[0]], "dom", split_axis=0, concat_axis=0, tiled=True)
-    hub_block = lax.all_gather(scaled[hub_rows[0]], "dom", axis=0, tiled=True)
+    hub_block = cube_test(scaled[hub_rows[0]])
     source = jnp.concatenate([scaled, arrived.reshape(-1, feature_width), hub_block], 0)
     source_blocks = source.shape[0] // tile_size
     source = source.reshape(source_blocks, tile_size, feature_width)

time: 283 us -> 305 us (1.078)
  waiting for transfers between devices: 135 us -> 199 us
  blocking collectives: 50.6 us -> 0 us
  starting transfers between devices: 29.1 us -> 36.1 us
    unnamed x4, waiting for transfers between devices: 92.1 us -> 146 us
    all_gather x1 -> x0, blocking collectives: 50.6 us -> none  [body(): hub_block = lax.all_gather(scaled[hub_rows[0]], 'dom', axis=0, tiled=True)]
    all_to_all x0 -> x1, starting transfers between devices: none -> 17.4 us  [edit_figure(): lax.all_to_all(jnp.stack([original for _ in range(lax.axis_size(lane_axis...]
    all_to_all x1, waiting for transfers between devices: 0.01 us -> 7.85 us  [body(): lax.all_to_all(scaled[send_rows[0]], 'dom', split_axis=0, concat_axis=0,...]
    all_to_all x1, starting transfers between devices: 17.8 us -> 11.9 us  [body(): lax.all_to_all(scaled[send_rows[0]], 'dom', split_axis=0, concat_axis=0,...]
    all_to_all x1, starting transfers between devices: 11 us -> 6.45 us  [body(): lax.all_to_all(boundary_part, 'dom', split_axis=0, concat_axis=0, tiled=T...]
  transfers between devices with their start and end apart: 5 -> 6, of which waited for: 3 -> 5; matrix products, arithmetic and copies ran while one was open for 13% -> 15% of each run, Pallas kernels for 0% -> 0%
where the time goes in v1:
time: 305 us
  waiting for transfers between devices  199 us (65%)
  starting transfers between devices  36.1 us (12%)
  local copies, waits for them, and re-layouts  22.8 us (7%)
  other arithmetic  19.3 us (6%)
  between operations  17 us (6%)
  matrix products  10.7 us (4%)
    unnamed x4, waiting for transfers between devices  146 us
    reduce_scatter x1, waiting for transfers between devices, body(): lax.psum_scatter(gradient_part, 'rep', scatter_dimension=0, tiled=True)  25 us
    all_to_all x1, waiting for transfers between devices, body(): lax.all_to_all(boundary_part, 'dom', split_axis=0, concat_axis=0, tiled=T...  17.9 us
    all_to_all x1, starting transfers between devices, edit_figure(): lax.all_to_all(jnp.stack([original for _ in range(lax.axis_size(lane_axis...  17.4 us
    scatter-add x1, other arithmetic, body(): gradient_part = local_part.at[send_rows[0]].add(returned)  12 us
    all_to_all x1, starting transfers between devices, body(): lax.all_to_all(scaled[send_rows[0]], 'dom', split_axis=0, concat_axis=0,...  11.9 us
    gather x1, local copies, waits for them, and re-layouts, body(): scaled[send_rows[0]]  7.98 us
    all_to_all x1, waiting for transfers between devices, body(): lax.all_to_all(scaled[send_rows[0]], 'dom', split_axis=0, concat_axis=0,...  7.85 us
  transfers between devices with their start and end apart: 6, of which 5 were waited for; matrix products, arithmetic and copies ran while one was open for 15% of the time, Pallas kernels for 0%

profile of v1, /device:TPU:8, one launch (start us, length us, event | category | flops | bytes accessed | tf_op | source)
XLA Modules:
  0.0 304.7 jit_solution(4639242432272159885)
XLA Ops:
  8.0 0.8 convert_rsqrt_fusion
  8.8 0.7 fusion.18
  9.5 1.2 multiply_convert_fusion
  11.3 0.7 stack.2
  12.0 17.4 %all-to-all-start.1 = ((bf16[128,4,128]{2,1,0:T(4,128)(2,1)}), bf16[128,4,128]{2,1,0:T(4,128)(2,1)S(1)}, u32[]{:S(2)}, u32[]{:S(2)}) async-start(bf16[128,4,128]{2,1,0:T(4,128)(2,1)} %stack.2), calls=%async_computation.1 | async-start | bytes 262144 | tf_op jit(solution)/shard_map/all_to_all | solution.py:10
  29.3 0.7 compare_select_fusion
  30.2 8.0 %gather_fusion = bf16[2048,128]{1,0:T(8,128)(2,1)} fusion(bf16[1024,128]{1,0:T(8,128)(2,1)S(1)} %get-tuple-element.3, s32[2048]{0:T(1024)S(1)} %broadcast_clamp_fusion), kind=kCustom, calls=%fused_computation | custom fusion | bytes 1056768 | tf_op jit(solution)/shard_map/gather | solution.py:41
  38.2 0.7 gather_fusion.3
  39.0 2.3 all-to-all-done.1
  41.3 11.9 %all-to-all-start = ((bf16[128,16,128]{2,1,0:T(8,128)(2,1)}), bf16[128,16,128]{2,1,0:T(8,128)(2,1)}, u32[]{:S(2)}, u32[]{:S(2)}) async-start(bf16[128,16,128]{2,1,0:T(8,128)(2,1)} %bitcast.3), calls=%async_computation | async-start | bytes 1048576 | tf_op jit(solution)/shard_map/all_to_all | solution.py:41
  53.3 1.8 convolution_bitcast_fusion
  55.1 1.9 copy.20
  57.7 3.7 %fusion = f32[28,16384]{1,0:T(8,128)S(1)} fusion(f32[4,8,128,128]{3,2,1,0:T(8,128)S(1)} %bitcast.46, f32[32]{0:T(128)S(1)} %compare_convert_fusion, s32[32]{0:T(128)} %bitcast.51), kind=kOutput, calls=%fused_computation.6 | convolution fusion | flops 176162560 | bytes 3932416 | tf_op jit(solution)/shard_map/dot_general | solution.py:75
  61.4 1.3 copy-done.2
  62.7 0.9 slice.20
  64.1 1.1 reshape.163
  65.2 7.9 %all-to-all-done = bf16[128,16,128]{2,1,0:T(8,128)(2,1)} async-done(((bf16[128,16,128]{2,1,0:T(8,128)(2,1)}), bf16[128,16,128]{2,1,0:T(8,128)(2,1)}, u32[]{:S(2)}, u32[]{:S(2)}) %all-to-all-start) | async-done | bytes 524320 | tf_op jit(solution)/shard_map/all_to_all | solution.py:41
  73.0 6.4 %all-to-all-start.2 = ((f32[128,16,128]{2,1,0:T(8,128)}), f32[128,16,128]{2,1,0:T(8,128)}, u32[]{:S(2)}, u32[]{:S(2)}) async-start(f32[128,16,128]{2,1,0:T(8,128)} %reshape.163), calls=%async_computation.3 | async-start | bytes 2097152 | tf_op jit(solution)/shard_map/all_to_all | solution.py:85
  79.7 1.1 pad_maximum_fusion
  80.8 0.7 gather_fusion.2
  81.6 2.2 convolution_bitcast_fusion.1
  83.8 1.9 copy.18
  85.7 3.0 fusion.3
  88.8 2.0 reshape.160
  91.0 1.3 dynamic-slice
  92.9 17.9 %all-to-all-done.2 = f32[128,16,128]{2,1,0:T(8,128)} async-done(((f32[128,16,128]{2,1,0:T(8,128)}), f32[128,16,128]{2,1,0:T(8,128)}, u32[]{:S(2)}, u32[]{:S(2)}) %all-to-all-start.2) | async-done | bytes 1048608 | tf_op jit(solution)/shard_map/all_to_all | solution.py:85
  110.8 12.0 %scatter_fusion = f32[1024,128]{1,0:T(8,128)S(1)} fusion(f32[1024,128]{1,0:T(8,128)S(1)} %slice.17, s32[2048]{0:T(1024)S(1)} %reshape.166, f32[2048,128]{1,0:T(8,128)} %bitcast.18), kind=kCustom, calls=%fused_computation.4 | custom fusion | flops 262144 | bytes 3153920 | tf_op jit(solution)/shard_map/scatter-add | solution.py:86
  122.9 145.8 %all-reduce.3.cloned.1.call-done = f32[512,128]{1,0:T(8,128)} async-done(((f32[512,128]{1,0:T(8,128)}), f32[512,128]{1,0:T(8,128)}) %all-reduce.3.cloned.1.call-update) | async-done | bytes 262160
  268.7 1.0 scatter_custom_fusion.1
  269.7 0.8 copy-done.1
  270.6 25.0 %reduce-scatter.5.cloned.1.call-done = f32[256,128]{1,0:T(8,128)} async-done(((f32[1024,128]{1,0:T(8,128)}), f32[256,128]{1,0:T(8,128)}) %reduce-scatter.5.cloned.1.call-update) | async-done | bytes 131088 | tf_op jit(solution)/shard_map/reduce_scatter | solution.py:91
  295.6 1.7 multiply_convert_fusion.2
  (36 shorter events, 1.8 us)
Async XLA Ops:
  8.0 45.3 %copy-start = (bf16[1,1,32,128,128]{4,3,2,1,0:T(8,128)(2,1)S(1)}, bf16[1,1,32,128,128]{4,3,2,1,0:T(8,128)(2,1)}, u32[]{:S(2)}) copy-start(bf16[1,1,32,128,128]{4,3,2,1,0:T(8,128)(2,1)} %param.12) | copy-start | bytes 3145732
  9.5 1.3 copy-start.6
  12.0 29.3 %all-to-all-start.1 = ((bf16[128,4,128]{2,1,0:T(4,128)(2,1)}), bf16[128,4,128]{2,1,0:T(4,128)(2,1)S(1)}, u32[]{:S(2)}, u32[]{:S(2)}) async-start(bf16[128,4,128]{2,1,0:T(4,128)(2,1)} %stack.2), calls=%async_computation.1 | async-start | bytes 262144 | tf_op jit(solution)/shard_map/all_to_all | solution.py:10
  30.2 8.0 %copy-start.4 = (s32[1,1,32]{2,1,0:T(1,128)S(1)}, s32[1,1,32]{2,1,0:T(1,128)}, u32[]{:S(2)}) copy-start(s32[1,1,32]{2,1,0:T(1,128)} %param.13) | copy-start | bytes 388
  41.3 31.8 %all-to-all-start = ((bf16[128,16,128]{2,1,0:T(8,128)(2,1)}), bf16[128,16,128]{2,1,0:T(8,128)(2,1)}, u32[]{:S(2)}, u32[]{:S(2)}) async-start(bf16[128,16,128]{2,1,0:T(8,128)(2,1)} %bitcast.3), calls=%async_computation | async-start | bytes 1048576 | tf_op jit(solution)/shard_map/all_to_all | solution.py:41
  53.2 215.5 %all-reduce.3.cloned.1.call-start = ((), (), s32[]{:S(2)}) async-start(), calls=%async_computation.7 | async-start | bytes 524288
  61.4 1.3 copy-start.2
  62.7 1.3 slice-start
  63.7 1.5 copy-start.3
  73.0 37.8 %all-to-all-start.2 = ((f32[128,16,128]{2,1,0:T(8,128)}), f32[128,16,128]{2,1,0:T(8,128)}, u32[]{:S(2)}, u32[]{:S(2)}) async-start(f32[128,16,128]{2,1,0:T(8,128)} %reshape.163), calls=%async_computation.3 | async-start | bytes 2097152 | tf_op jit(solution)/shard_map/all_to_all | solution.py:85
  79.5 191.1 %reduce-scatter.3.cloned.1.call-start = ((), (), s32[]{:S(2)}) async-start(), calls=%async_computation.5 | async-start | bytes 655360 | tf_op jit(solution)/shard_map/reduce_scatter | solution.py:90
  83.8 1.9 copy-start.5
  88.8 2.1 slice-start.1
  90.8 204.8 %reduce-scatter.5.cloned.1.call-start = ((), (), s32[]{:S(2)}) async-start(), calls=%async_computation.6 | async-start | bytes 655360 | tf_op jit(solution)/shard_map/reduce_scatter | solution.py:91
  269.7 0.8 copy-start.1
Sparse Core Ops, SparseCore 0:
  63.8 204.8 all-reduce.2
Sparse Core Ops, SparseCore 1:
  90.9 27.8 reduce-scatter.2
  270.6 25.0 reduce-scatter.4
